TPU v7x, 32 devices: a whole 2x2x4 slice. The times are simulated.
32 devices in a mesh: layer: 16 (over z, y, core), dp: 2 (over x).
Axes of the slice: x: 2, y: 2, z: 4, core: 2. Of those that a mesh axis runs over, the one named last changes fastest.
Arguments:
- c_guess: float32 [16, 256, 512], P('layer', 'dp'), may hold values from -6 to 6
- adj_guess: float32 [16, 256, 512], P('layer', 'dp'), may hold values from -6 to 6
- norm_gain: float32 [32, 512], P('layer'), may hold values from 0.5 to 1.5
- w_up: bfloat16 [32, 512, 2048], P('layer'), may hold values from -0.25 to 0.25
- w_down: bfloat16 [32, 2048, 512], P('layer'), may hold values from -0.125 to 0.125
- coarse_rate: float32 [16, 512], P('layer'), may hold values from 0.5 to 1
Outputs:
- c_points: float32 [16, 256, 512], P('layer', 'dp')
- adj_points: float32 [16, 256, 512], P('layer', 'dp')
- grad_up: float32 [32, 512, 2048], P('layer', 'dp')
- grad_down: float32 [32, 2048, 512], P('layer', 'dp')
All inputs are finite; a program needn't handle non-finite values.
Results may differ from a plain program's by a relative error of at most 0.018.
Values may be sent and summed in bfloat16 or wider, within the bound.
A program may use at most 64 MiB of HBM per device.

v0:
```python
import jax
import jax.numpy as jnp
from jax import lax
from jax.sharding import PartitionSpec as P

eps = 1e-06
step_length = 0.5


def carried_in(x, axis, combine, identity, reverse):
    size, here = (lax.axis_size(axis), lax.axis_index(axis))
    everything = jax.tree.map(lambda part: lax.all_gather(part, axis), x)
    start = jax.tree.map(
        lambda part, zero: jnp.broadcast_to(jnp.asarray(zero, part.dtype), part.shape), x, identity
    )

    def step(k, before):
        at = size - 1 - k if reverse else k
        reached = at > here if reverse else at < here
        new = combine(before, jax.tree.map(lambda part: part[at], everything))
        return jax.tree.map(lambda a, b: jnp.where(reached, a, b), new, before)

    return lax.fori_loop(0, size, step, start)


def normalize(state):
    inverse_rms = lax.rsqrt(jnp.mean(state * state, axis=-1, keepdims=True) + eps)
    return (state * inverse_rms, inverse_rms)


def layer_forward(state, gain_row, up_matrix, down_matrix):
    unit_state, inverse_rms = normalize(state)
    normed = (unit_state * gain_row).astype(jnp.bfloat16)
    preact = jnp.dot(normed, up_matrix, preferred_element_type=jnp.float32)
    hidden = jax.nn.silu(preact).astype(jnp.bfloat16)
    return state + step_length * jnp.dot(hidden, down_matrix, preferred_element_type=jnp.float32)


def layer_backward(state, cotangent, gain_row, up_matrix, down_matrix):
    unit_state, inverse_rms = normalize(state)
    normed = (unit_state * gain_row).astype(jnp.bfloat16)
    preact = jnp.dot(normed, up_matrix, preferred_element_type=jnp.float32)
    hidden = jax.nn.silu(preact).astype(jnp.bfloat16)
    sigmoid_pre = jax.nn.sigmoid(preact)
    out_grad = (step_length * cotangent).astype(jnp.bfloat16)
    hidden_grad = jnp.dot(out_grad, down_matrix.T, preferred_element_type=jnp.float32)
    pre_grad = (hidden_grad * sigmoid_pre * (1.0 + preact * (1.0 - sigmoid_pre))).astype(
        jnp.bfloat16
    )
    normed_grad = jnp.dot(pre_grad, up_matrix.T, preferred_element_type=jnp.float32)
    unit_grad = normed_grad * gain_row
    inner = jnp.mean(unit_grad * unit_state, axis=-1, keepdims=True)
    new_cotangent = cotangent + inverse_rms * (unit_grad - unit_state * inner)
    return (new_cotangent, normed, pre_grad, hidden, out_grad)


def block_forward(state, gains, ups, downs):
    for depth_index in range(gains.shape[0]):
        state = layer_forward(state, gains[depth_index], ups[depth_index], downs[depth_index])
    return state


def block_inputs(state, gains, ups, downs):
    inputs = [state]
    state = layer_forward(state, gains[0], ups[0], downs[0])
    inputs.append(state)
    return inputs


def block_backward(inputs, cotangent, gains, ups, downs):
    normed_list, pre_list, hidden_list, out_list = ([], [], [], [])
    for depth_index in reversed(range(gains.shape[0])):
        cotangent, normed, pre_grad, hidden, out_grad = layer_backward(
            inputs[depth_index], cotangent, gains[depth_index], ups[depth_index], downs[depth_index]
        )
        normed_list.insert(0, normed)
        pre_list.insert(0, pre_grad)
        hidden_list.insert(0, hidden)
        out_list.insert(0, out_grad)
    factors = (
        jnp.stack(normed_list),
        jnp.stack(pre_list),
        jnp.stack(hidden_list),
        jnp.stack(out_list),
    )
    return (cotangent, factors)


def compose(earlier, later):
    return (earlier[0] * later[0], later[0] * earlier[1] + later[1])


def shards(c_guess, adj_guess, norm_gain, w_up, w_down, coarse_rate):
    position = lax.axis_index("layer")
    devices = lax.axis_size("layer")
    leading = position == 0
    trailing = position == devices - 1
    start_state = c_guess[0]
    decay_rate = coarse_rate[0]
    identity_map = (jnp.ones_like(decay_rate), jnp.zeros_like(start_state))
    block_end = block_forward(start_state, norm_gain, w_up, w_down)
    forward_rate = jnp.where(leading, jnp.zeros_like(decay_rate), decay_rate)
    forward_shift = block_end - forward_rate * start_state
    _, carried = carried_in((forward_rate, forward_shift), "layer", compose, identity_map, False)
    point = jnp.where(leading, start_state, carried)
    inputs = block_inputs(point, norm_gain, w_up, w_down)
    adjoint_guess = adj_guess[0]
    begin, _ = block_backward(inputs, adjoint_guess, norm_gain, w_up, w_down)
    backward_rate = jnp.where(trailing, jnp.zeros_like(decay_rate), decay_rate)
    backward_shift = begin - backward_rate * adjoint_guess
    _, carried_back = carried_in(
        (backward_rate, backward_shift), "layer", compose, identity_map, True
    )
    adjoint = jnp.where(trailing, adjoint_guess, carried_back)
    _, factors = block_backward(inputs, adjoint, norm_gain, w_up, w_down)
    normed_all, pre_all, hidden_all, out_all = factors
    group = lax.axis_size("dp")
    member = lax.axis_index("dp")
    width_share = w_up.shape[1] // group
    hidden_share = w_up.shape[2] // group
    piece_normed = lax.all_gather(normed_all, "dp", axis=1, tiled=True)
    piece_pre = lax.all_gather(pre_all, "dp", axis=1, tiled=True)
    piece_hidden = lax.all_gather(hidden_all, "dp", axis=1, tiled=True)
    piece_out = lax.all_gather(out_all, "dp", axis=1, tiled=True)
    normed_cols = lax.dynamic_slice_in_dim(piece_normed, member * width_share, width_share, 2)
    hidden_cols = lax.dynamic_slice_in_dim(piece_hidden, member * hidden_share, hidden_share, 2)
    up_part = jnp.einsum("ltd,ltf->ldf", normed_cols, piece_pre, preferred_element_type=jnp.float32)
    down_part = jnp.einsum(
        "ltf,ltd->lfd", hidden_cols, piece_out, preferred_element_type=jnp.float32
    )
    return (point[None], adjoint[None], up_part, down_part)


def solution(mesh):
    return jax.shard_map(
        shards,
        mesh=mesh,
        in_specs=(
            P("layer", "dp", None),
            P("layer", "dp", None),
            P("layer", None),
            P("layer", None, None),
            P("layer", None, None),
            P("layer", None),
        ),
        out_specs=(
            P("layer", "dp", None),
            P("layer", "dp", None),
            P("layer", "dp", None),
            P("layer", "dp", None),
        ),
        check_vma=False,
    )
```

profile of v0, /device:TPU:0, one launch (start us, length us, event | category | flops | bytes accessed | tf_op | source)
XLA Modules:
  0.0 239.0 jit_solution(10892800529612794329)
XLA Ops:
  9.1 3.2 %multiply_reduce_fusion.5 = (f32[128]{0:T(128)S(1)}, f32[128,512]{1,0:T(8,128)S(1)}) fusion(bf16[2,2048,512]{2,1,0:T(8,128)(2,1)} %param.14, bf16[2,512,2048]{2,1,0:T(8,128)(2,1)} %param.13, f32[1,128,512]{2,1,0:T(8,128)} %param.10, f32[512]{0:T(512)S(1)} %bitcast.178, f32[128]{0:T(128)S(1)} %add_rsqrt_fusion.3), kind=kOutput, calls=%fused_computation.108 | convolution fusion | flops 538640256 | bytes 4983808 | tf_op jit(solution)/shard_map/dot_general | solution.py:36
  12.3 3.7 %fusion.76 = f32[128,512]{1,0:T(8,128)} fusion(f32[128,512]{1,0:T(8,128)S(1)} %get-tuple-element.301, bf16[2,2048,512]{2,1,0:T(8,128)(2,1)} %param.14, bf16[2,512,2048]{2,1,0:T(8,128)(2,1)} %param.13, f32[1,128,512]{2,1,0:T(8,128)S(1)} %copy-done.3, f32[512]{0:T(512)S(1)} %bitcast.184, f32[512]{0:T(512)S(1)} %bitcast.173, f32[128]{0:T(128)S(1)} %add_rsqrt_fusion.2), kind=kOutput, calls=%fused_computation.66 | convolution fusion | flops 538640384 | bytes 5247488 | tf_op jit(solution)/shard_map/dot_general | solution.py:36
  16.1 23.3 %all-gather.2 = f32[16,1,512]{2,1,0:T(1,128)S(1)} all-gather(f32[1,1,512]{2,1,0:T(1,128)S(1)} %bitcast.185), channel_id=1, replica_groups=mesh['layer'=16,'dp'=2] {'layer'}, dimensions={0}, use_global_device_ids=true | all-gather | bytes 34816 | tf_op jit(solution)/shard_map/all_gather | solution.py:12
  39.4 29.9 %all-gather.13.cloned.1.call-done = f32[2048,512]{1,0:T(8,128)} async-done(((f32[128,512]{1,0:T(8,128)}), f32[2048,512]{1,0:T(8,128)}) %all-gather.13.cloned.1.call-update) | async-done | bytes 4194320 | tf_op jit(solution)/shard_map/all_gather | solution.py:12
  69.3 19.1 %while.30 = (s32[]{:T(128)}, f32[128,512]{1,0:T(8,128)S(1)}, s32[]{:T(128)}, f32[16,512]{1,0:T(8,128)S(1)}, f32[16,128,512]{2,1,0:T(8,128)}, /*index=5*/s32[]{:T(128)}, s32[]{:T(128)}) while((s32[]{:T(128)}, f32[128,512]{1,0:T(8,128)S(1)}, s32[]{:T(128)}, f32[16,512]{1,0:T(8,128)S(1)}, f32[16,128,512]{2,1,0:T(8,128)}, ...), condition=%wide.region_3.4_spmd.clone, body=%wide.region_2.3_spmd.clone.sunk | while | flops 262148 | bytes 792689 | solution.py:23
  70.5 1.2 fusion.150
  88.6 2.2 fusion.31
  92.0 1.5 copy-done.1
  94.1 4.5 %multiply_reduce_fusion.2 = (f32[128]{0:T(128)S(1)}, f32[128,512]{1,0:T(8,128)}) fusion(f32[128,512]{1,0:T(8,128)S(1)} %get-tuple-element.303, f32[128]{0:T(128)S(1)} %add_rsqrt_fusion, f32[512]{0:T(512)S(1)} %bitcast.175, bf16[2,512,2048]{2,1,0:T(8,128)(2,1)} %param.13, bf16[2,2048,512]{2,1,0:T(8,128)(2,1)} %param.14, f32[128,2048]{1,0:T(8,128)S(1)} %fusion.19, ...), kind=kOutput, calls=%fused_computation.101 | convolution fusion | flops 539623296 | bytes 6032384 | tf_op jit(solution)/shard_map/dot_general | solution.py:50
  98.6 3.9 %fusion.49 = f32[128,512]{1,0:T(8,128)S(1)} fusion(bf16[2,512,2048]{2,1,0:T(8,128)(2,1)} %param.13, bf16[2,2048,512]{2,1,0:T(8,128)(2,1)} %param.14, f32[128,2048]{1,0:T(8,128)S(1)} %fusion.31, f32[512]{0:T(512)S(1)} %bitcast.180, f32[1,128,512]{2,1,0:T(8,128)S(1)} %copy-done.4, f32[128,512]{1,0:T(8,128)} %get-tuple-element.305, ...), kind=kOutput, calls=%fused_computation.57 | convolution fusion | flops 539754496 | bytes 6294528 | tf_op jit(solution)/shard_map/dot_general | solution.py:50
  102.7 1.8 fusion.133
  104.6 19.1 %all-gather.3 = f32[16,1,512]{2,1,0:T(1,128)S(1)} all-gather(f32[1,1,512]{2,1,0:T(1,128)S(1)} %bitcast.183), channel_id=1, replica_groups=mesh['layer'=16,'dp'=2] {'layer'}, dimensions={0}, use_global_device_ids=true | all-gather | bytes 34816 | tf_op jit(solution)/shard_map/all_gather | solution.py:12
  125.4 28.2 %all-gather.15.cloned.1.call-done = f32[2048,512]{1,0:T(8,128)} async-done(((f32[128,512]{1,0:T(8,128)}), f32[2048,512]{1,0:T(8,128)}) %all-gather.15.cloned.1.call-update) | async-done | bytes 4194320 | tf_op jit(solution)/shard_map/all_gather | solution.py:12
  153.7 19.3 %while.31 = (s32[]{:T(128)}, f32[128,512]{1,0:T(8,128)S(1)}, s32[]{:T(128)}, f32[16,512]{1,0:T(8,128)S(1)}, f32[16,128,512]{2,1,0:T(8,128)}, /*index=5*/s32[]{:T(128)}, s32[]{:T(128)}, s32[]{:T(128)}, s32[]{:T(128)}) while((s32[]{:T(128)}, f32[128,512]{1,0:T(8,128)S(1)}, s32[]{:T(128)}, f32[16,512]{1,0:T(8,128)S(1)}, ...), condition=%wide.region_9.10_spmd.clone, body=%wide.region_8.9_spmd.clone.sunk | while | flops 262152 | bytes 792751 | solution.py:23
  159.7 1.2 fusion.151
  160.9 1.2 fusion.151
  162.1 1.2 fusion.151
  163.3 1.2 fusion.151
  173.0 2.6 %fusion.8 = bf16[128,2048]{1,0:T(8,128)(2,1)S(1)} fusion(bf16[2,2048,512]{2,1,0:T(8,128)(2,1)} %param.14, f32[128,2048]{1,0:T(8,128)S(1)} %fusion.19, f32[128,512]{1,0:T(8,128)S(1)} %get-tuple-element.289), kind=kOutput, calls=%fused_computation.16 | convolution fusion | flops 270925824 | bytes 3932160 | tf_op jit(solution)/shard_map/dot_general | solution.py:46
  180.2 12.6 %all_gather.38 = bf16[2,256,512]{2,1,0:T(8,128)(2,1)S(1)} all-gather(bf16[2,128,512]{2,1,0:T(8,128)(2,1)S(1)} %pad_maximum_fusion.2), channel_id=1, replica_groups=mesh['layer'=16,'dp'=2] {'dp'}, dimensions={1}, use_global_device_ids=true | all-gather | bytes 786432 | tf_op jit(solution)/shard_map/all_gather | solution.py:121
  192.8 8.8 %all_gather.41 = bf16[2,256,512]{2,1,0:T(8,128)(2,1)S(1)} all-gather(bf16[2,128,512]{2,1,0:T(8,128)(2,1)S(1)} %pad_maximum_fusion.3), channel_id=1, replica_groups=mesh['layer'=16,'dp'=2] {'dp'}, dimensions={1}, use_global_device_ids=true | all-gather | bytes 786432 | tf_op jit(solution)/shard_map/all_gather | solution.py:124
  201.6 4.1 %fusion.79 = f32[2,1024,512]{2,1,0:T(8,128)} fusion(bf16[2,256,512]{2,1,0:T(8,128)(2,1)S(1)} %all_gather.41, bf16[2,256,2048]{2,1,0:T(8,128)(2,1)} %all-gather.11.cloned.1.call-done, s32[]{:T(128)S(6)} %select_n.96), kind=kOutput, calls=%fused_computation.69 | convolution fusion | flops 536870912 | bytes 5767172 | tf_op jit(solution)/shard_map/ltf,ltd->lfd/dot_general | solution.py:128
  205.7 22.4 %all-gather.9.cloned.1.call-done = bf16[2,256,2048]{2,1,0:T(8,128)(2,1)} async-done(((bf16[2,128,2048]{2,1,0:T(8,128)(2,1)}), bf16[2,256,2048]{2,1,0:T(8,128)(2,1)}) %all-gather.9.cloned.1.call-update) | async-done | bytes 2097168 | tf_op jit(solution)/shard_map/all_gather | solution.py:122
  228.1 4.4 %fusion.100 = f32[2,256,2048]{2,1,0:T(8,128)} fusion(bf16[2,256,2048]{2,1,0:T(8,128)(2,1)} %all-gather.9.cloned.1.call-done, bf16[2,256,512]{2,1,0:T(8,128)(2,1)S(1)} %all_gather.38, s32[]{:T(128)S(6)} %select_n.95), kind=kOutput, calls=%fused_computation.97 | convolution fusion | flops 536870912 | bytes 6553604 | tf_op jit(solution)/shard_map/ltd,ltf->ldf/dot_general | solution.py:127
  (112 shorter events, 41.8 us)
Async XLA Ops:
  7.2 62.2 %all-gather.13.cloned.1.call-start = ((), (), s32[]{:S(2)}) async-start(), calls=%async_computation.2 | async-start | bytes 4456448 | tf_op jit(solution)/shard_map/all_gather | solution.py:12
  9.1 3.2 %copy-start.6 = (f32[1,512]{1,0:T(1,128)S(1)}, f32[1,512]{1,0:T(1,128)}, u32[]{:S(2)}) copy-start(f32[1,512]{1,0:T(1,128)} %param.15) | copy-start | bytes 6148
  9.1 3.2 %copy-start.3 = (f32[1,128,512]{2,1,0:T(8,128)S(1)}, f32[1,128,512]{2,1,0:T(8,128)}, u32[]{:S(2)}) copy-start(f32[1,128,512]{2,1,0:T(8,128)} %param.10) | copy-start | bytes 786436
  16.1 137.6 %all-gather.15.cloned.1.call-start = ((), (), s32[]{:S(2)}) async-start(), calls=%async_computation.3 | async-start | bytes 4456448 | tf_op jit(solution)/shard_map/all_gather | solution.py:12
  88.5 2.9 %copy-start.7 = (bf16[2,2048,512]{2,1,0:T(8,128)(2,1)S(1)}, bf16[2,2048,512]{2,1,0:T(8,128)(2,1)}, u32[]{:S(2)}) copy-start(bf16[2,2048,512]{2,1,0:T(8,128)(2,1)} %param.14) | copy-start | bytes 12582916
  88.6 14.0 %copy-start = (f32[128,512]{1,0:T(8,128)}, f32[128,512]{1,0:T(8,128)S(1)}, u32[]{:S(2)}) copy-start(f32[128,512]{1,0:T(8,128)S(1)} %get-tuple-element.291) | copy-start | bytes 786436
  91.4 2.2 copy-start.1
  91.4 2.7 %copy-start.4 = (f32[1,128,512]{2,1,0:T(8,128)S(1)}, f32[1,128,512]{2,1,0:T(8,128)}, u32[]{:S(2)}) copy-start(f32[1,128,512]{2,1,0:T(8,128)} %param.11) | copy-start | bytes 786436
  104.5 97.1 %all-gather.11.cloned.1.call-start = ((), (), s32[]{:S(2)}) async-start(), calls=%async_computation.1 | async-start | bytes 3145728 | tf_op jit(solution)/shard_map/all_gather | solution.py:123
  125.4 102.8 %all-gather.9.cloned.1.call-start = ((), (), s32[]{:S(2)}) async-start(), calls=%async_computation | async-start | bytes 3145728 | tf_op jit(solution)/shard_map/all_gather | solution.py:122
  173.0 3.9 %copy-start.5 = (f32[128,512]{1,0:T(8,128)}, f32[128,512]{1,0:T(8,128)S(1)}, u32[]{:S(2)}) copy-start(f32[128,512]{1,0:T(8,128)S(1)} %get-tuple-element.289) | copy-start | bytes 786436
  173.0 2.9 %copy-start.2 = (bf16[2,512,2048]{2,1,0:T(8,128)(2,1)S(1)}, bf16[2,512,2048]{2,1,0:T(8,128)(2,1)}, u32[]{:S(2)}) copy-start(bf16[2,512,2048]{2,1,0:T(8,128)(2,1)} %param.13) | copy-start | bytes 12582916
  175.9 2.2 copy-start.8
Sparse Core Ops, SparseCore 0:
  16.2 53.0 all-gather.12
  104.6 48.9 all-gather.14
  155.8 35.1 all-gather.10
  192.9 35.1 all-gather.8
where the time goes:
time: 240 us; the launch traced here: 239 us
  waiting for transfers between devices  80.6 us (34%)
  blocking collectives  63.9 us (27%)
  other arithmetic  43.3 us (18%)
  matrix products  31.5 us (13%)
  between operations  14 us (6%)
  local copies, waits for them, and re-layouts  4.58 us (2%)
    all_gather x2, waiting for transfers between devices, carried_in(): everything = jax.tree.map(lambda part: lax.all_gather(part, axis), x)  58.1 us
    all_gather x2, blocking collectives, carried_in(): everything = jax.tree.map(lambda part: lax.all_gather(part, axis), x)  42.4 us
    select_n x32, other arithmetic, step(): return jax.tree.map(lambda a, b: jnp.where(reached, a, b), new, before)  37.1 us
    all_gather x1, waiting for transfers between devices, shards(): piece_pre = lax.all_gather(pre_all, 'dp', axis=1, tiled=True)  22.4 us
    all_gather x1, blocking collectives, shards(): piece_normed = lax.all_gather(normed_all, 'dp', axis=1, tiled=True)  12.6 us
    dot_general x3, matrix products, layer_backward(): jnp.dot(pre_grad, up_matrix.T, preferred_element_type=jnp.float32)  9.26 us
    all_gather x1, blocking collectives, shards(): piece_out = lax.all_gather(out_all, 'dp', axis=1, tiled=True)  8.79 us
    dot_general x3, matrix products, layer_forward(): jnp.dot(hidden, down_matrix, preferred_element_type=jnp.float32)  7.55 us
  transfers between devices with their start and end apart: 4, of which 3 were waited for; matrix products, arithmetic and copies ran while one was open for 13% of the time, Pallas kernels for 0%

commit v1 on v0

--- a/solution.py
+++ b/solution.py
@@ -119,7 +119,8 @@
     width_share = w_up.shape[1] // group
     hidden_share = w_up.shape[2] // group
     piece_normed = lax.all_gather(normed_all, "dp", axis=1, tiled=True)
-    piece_pre = lax.all_gather(pre_all, "dp", axis=1, tiled=True)
+    parts = lax.all_gather(pre_all, "dp")
+    piece_pre = jnp.concatenate(parts, axis=1)
     piece_hidden = lax.all_gather(hidden_all, "dp", axis=1, tiled=True)
     piece_out = lax.all_gather(out_all, "dp", axis=1, tiled=True)
     normed_cols = lax.dynamic_slice_in_dim(piece_normed, member * width_share, width_share, 2)

time: 240 us -> 241 us (level)
  local copies, waits for them, and re-layouts: 4.58 us -> 7.01 us
where the time goes in v1:
time: 241 us; the launch traced here: 239 us
  waiting for transfers between devices  80.6 us (33%)
  blocking collectives  63.8 us (26%)
  other arithmetic  43.3 us (18%)
  matrix products  29.2 us (12%)
  between operations  14 us (6%)
  local copies, waits for them, and re-layouts  7.01 us (3%)
    all_gather x2, waiting for transfers between devices, carried_in(): everything = jax.tree.map(lambda part: lax.all_gather(part, axis), x)  58.1 us
    all_gather x2, blocking collectives, carried_in(): everything = jax.tree.map(lambda part: lax.all_gather(part, axis), x)  42.4 us
    select_n x32, other arithmetic, step(): return jax.tree.map(lambda a, b: jnp.where(reached, a, b), new, before)  37.1 us
    all_gather x1, waiting for transfers between devices, shards(): parts = lax.all_gather(pre_all, 'dp')  22.4 us
    all_gather x1, blocking collectives, shards(): piece_normed = lax.all_gather(normed_all, 'dp', axis=1, tiled=True)  12.6 us
    all_gather x1, blocking collectives, shards(): piece_out = lax.all_gather(out_all, 'dp', axis=1, tiled=True)  8.79 us
    dot_general x3, matrix products, layer_backward(): jnp.dot(pre_grad, up_matrix.T, preferred_element_type=jnp.float32)  8.56 us
    dot_general x3, matrix products, layer_forward(): jnp.dot(hidden, down_matrix, preferred_element_type=jnp.float32)  7.56 us
  transfers between devices with their start and end apart: 4, of which 3 were waited for; matrix products, arithmetic and copies ran while one was open for 13% of the time, Pallas kernels for 0%

profile of v1, /device:TPU:0, one launch (start us, length us, event | category | flops | bytes accessed | tf_op | source)
XLA Modules:
  0.0 239.2 jit_solution(5272726084246386224)
XLA Ops:
  9.1 3.2 %multiply_reduce_fusion.5 = (f32[128]{0:T(128)S(1)}, f32[128,512]{1,0:T(8,128)S(1)}) fusion(bf16[2,2048,512]{2,1,0:T(8,128)(2,1)} %param.14, bf16[2,512,2048]{2,1,0:T(8,128)(2,1)} %param.13, f32[1,128,512]{2,1,0:T(8,128)} %param.10, f32[512]{0:T(512)S(1)} %bitcast.184, f32[128]{0:T(128)S(1)} %add_rsqrt_fusion.3), kind=kOutput, calls=%fused_computation.108 | convolution fusion | flops 538640256 | bytes 4983808 | tf_op jit(solution)/shard_map/dot_general | solution.py:36
  12.3 3.7 %fusion.76 = f32[128,512]{1,0:T(8,128)} fusion(f32[128,512]{1,0:T(8,128)S(1)} %get-tuple-element.301, bf16[2,2048,512]{2,1,0:T(8,128)(2,1)} %param.14, bf16[2,512,2048]{2,1,0:T(8,128)(2,1)} %param.13, f32[1,128,512]{2,1,0:T(8,128)S(1)} %copy-done.3, f32[512]{0:T(512)S(1)} %bitcast.190, f32[512]{0:T(512)S(1)} %bitcast.179, f32[128]{0:T(128)S(1)} %add_rsqrt_fusion.2), kind=kOutput, calls=%fused_computation.66 | convolution fusion | flops 538640384 | bytes 5247488 | tf_op jit(solution)/shard_map/dot_general | solution.py:36
  16.1 23.3 %all-gather.3 = f32[16,1,512]{2,1,0:T(1,128)S(1)} all-gather(f32[1,1,512]{2,1,0:T(1,128)S(1)} %bitcast.191), channel_id=1, replica_groups=mesh['layer'=16,'dp'=2] {'layer'}, dimensions={0}, use_global_device_ids=true | all-gather | bytes 34816 | tf_op jit(solution)/shard_map/all_gather | solution.py:12
  39.5 29.9 %all-gather.12.cloned.1.call-done = f32[2048,512]{1,0:T(8,128)} async-done(((f32[128,512]{1,0:T(8,128)}), f32[2048,512]{1,0:T(8,128)}) %all-gather.12.cloned.1.call-update) | async-done | bytes 4194320 | tf_op jit(solution)/shard_map/all_gather | solution.py:12
  69.3 19.1 %while.30 = (s32[]{:T(128)}, f32[128,512]{1,0:T(8,128)S(1)}, s32[]{:T(128)}, f32[16,512]{1,0:T(8,128)S(1)}, f32[16,128,512]{2,1,0:T(8,128)}, /*index=5*/s32[]{:T(128)}, s32[]{:T(128)}) while((s32[]{:T(128)}, f32[128,512]{1,0:T(8,128)S(1)}, s32[]{:T(128)}, f32[16,512]{1,0:T(8,128)S(1)}, f32[16,128,512]{2,1,0:T(8,128)}, ...), condition=%wide.region_3.4_spmd.clone, body=%wide.region_2.3_spmd.clone.sunk | while | flops 262148 | bytes 792689 | solution.py:23
  88.6 2.3 fusion.31
  92.0 1.5 copy-done.1
  94.1 3.9 %multiply_reduce_fusion.2 = (f32[128]{0:T(128)S(1)}, f32[128,512]{1,0:T(8,128)S(1)}) fusion(f32[128,512]{1,0:T(8,128)S(1)} %get-tuple-element.303, f32[128]{0:T(128)S(1)} %add_rsqrt_fusion, f32[512]{0:T(512)S(1)} %bitcast.181, bf16[2,512,2048]{2,1,0:T(8,128)(2,1)} %param.13, bf16[2,2048,512]{2,1,0:T(8,128)(2,1)} %param.14, f32[128,2048]{1,0:T(8,128)S(1)} %fusion.19, ...), kind=kOutput, calls=%fused_computation.101 | convolution fusion | flops 539623296 | bytes 6032384 | tf_op jit(solution)/shard_map/dot_general | solution.py:50
  98.6 3.8 %fusion.49 = f32[128,512]{1,0:T(8,128)S(1)} fusion(bf16[2,512,2048]{2,1,0:T(8,128)(2,1)} %param.13, bf16[2,2048,512]{2,1,0:T(8,128)(2,1)} %param.14, f32[128,2048]{1,0:T(8,128)S(1)} %fusion.31, f32[512]{0:T(512)S(1)} %bitcast.186, f32[1,128,512]{2,1,0:T(8,128)S(1)} %copy-done.4, f32[128,512]{1,0:T(8,128)S(1)} %get-tuple-element.305, ...), kind=kOutput, calls=%fused_computation.57 | convolution fusion | flops 539754496 | bytes 6294528 | tf_op jit(solution)/shard_map/dot_general | solution.py:50
  102.7 1.8 fusion.133
  104.6 19.1 %all-gather.4 = f32[16,1,512]{2,1,0:T(1,128)S(1)} all-gather(f32[1,1,512]{2,1,0:T(1,128)S(1)} %bitcast.189), channel_id=1, replica_groups=mesh['layer'=16,'dp'=2] {'layer'}, dimensions={0}, use_global_device_ids=true | all-gather | bytes 34816 | tf_op jit(solution)/shard_map/all_gather | solution.py:12
  125.4 28.3 %all-gather.14.cloned.1.call-done = f32[2048,512]{1,0:T(8,128)} async-done(((f32[128,512]{1,0:T(8,128)}), f32[2048,512]{1,0:T(8,128)}) %all-gather.14.cloned.1.call-update) | async-done | bytes 4194320 | tf_op jit(solution)/shard_map/all_gather | solution.py:12
  153.7 19.3 %while.31 = (s32[]{:T(128)}, f32[128,512]{1,0:T(8,128)S(1)}, s32[]{:T(128)}, f32[16,512]{1,0:T(8,128)S(1)}, f32[16,128,512]{2,1,0:T(8,128)}, /*index=5*/s32[]{:T(128)}, s32[]{:T(128)}, s32[]{:T(128)}, s32[]{:T(128)}) while((s32[]{:T(128)}, f32[128,512]{1,0:T(8,128)S(1)}, s32[]{:T(128)}, f32[16,512]{1,0:T(8,128)S(1)}, ...), condition=%wide.region_9.10_spmd.clone, body=%wide.region_8.9_spmd.clone.sunk | while | flops 262152 | bytes 792751 | solution.py:23
  159.7 1.2 fusion.151
  160.9 1.2 fusion.151
  162.2 1.2 fusion.151
  163.4 1.2 fusion.151
  173.1 2.6 %fusion.8 = bf16[128,2048]{1,0:T(8,128)(2,1)S(1)} fusion(bf16[2,2048,512]{2,1,0:T(8,128)(2,1)} %param.14, f32[128,2048]{1,0:T(8,128)S(1)} %fusion.19, f32[128,512]{1,0:T(8,128)S(1)} %get-tuple-element.289), kind=kOutput, calls=%fused_computation.16 | convolution fusion | flops 270925824 | bytes 3932160 | tf_op jit(solution)/shard_map/dot_general | solution.py:46
  180.2 12.6 %all_gather.41 = bf16[2,256,512]{2,1,0:T(8,128)(2,1)S(1)} all-gather(bf16[2,128,512]{2,1,0:T(8,128)(2,1)S(1)} %pad_maximum_fusion.2), channel_id=1, replica_groups=mesh['layer'=16,'dp'=2] {'dp'}, dimensions={1}, use_global_device_ids=true | all-gather | bytes 786432 | tf_op jit(solution)/shard_map/all_gather | solution.py:121
  192.8 8.8 %all_gather.45 = bf16[2,256,512]{2,1,0:T(8,128)(2,1)S(1)} all-gather(bf16[2,128,512]{2,1,0:T(8,128)(2,1)S(1)} %pad_maximum_fusion.3), channel_id=1, replica_groups=mesh['layer'=16,'dp'=2] {'dp'}, dimensions={1}, use_global_device_ids=true | all-gather | bytes 786432 | tf_op jit(solution)/shard_map/all_gather | solution.py:125
  201.6 4.1 %fusion.79 = f32[2,1024,512]{2,1,0:T(8,128)} fusion(bf16[2,256,512]{2,1,0:T(8,128)(2,1)S(1)} %all_gather.45, bf16[2,256,2048]{2,1,0:T(8,128)(2,1)} %all-gather.10.cloned.1.call-done, s32[]{:T(128)S(6)} %select_n.96), kind=kOutput, calls=%fused_computation.69 | convolution fusion | flops 536870912 | bytes 5767172 | tf_op jit(solution)/shard_map/ltf,ltd->lfd/dot_general | solution.py:129
  205.8 22.4 %all-gather.16.cloned.1.call-done = bf16[4,128,2048]{2,1,0:T(8,128)(2,1)} async-done(((bf16[2,128,2048]{2,1,0:T(8,128)(2,1)}), bf16[4,128,2048]{2,1,0:T(8,128)(2,1)}) %all-gather.16.cloned.1.call-update) | async-done | bytes 2097168 | tf_op jit(solution)/shard_map/all_gather | solution.py:122
  228.2 1.7 copy.13
  229.9 2.8 %fusion.100 = f32[2,256,2048]{2,1,0:T(8,128)} fusion(bf16[2,256,2048]{2,1,0:T(8,128)(2,1)S(1)} %bitcast.167, bf16[2,256,512]{2,1,0:T(8,128)(2,1)S(1)} %all_gather.41, s32[]{:T(128)S(6)} %select_n.95), kind=kOutput, calls=%fused_computation.97 | convolution fusion | flops 536870912 | bytes 6553604 | tf_op jit(solution)/shard_map/ltd,ltf->ldf/dot_general | solution.py:128
  (115 shorter events, 43.6 us)
Async XLA Ops:
  7.2 62.2 %all-gather.12.cloned.1.call-start = ((), (), s32[]{:S(2)}) async-start(), calls=%async_computation.1 | async-start | bytes 4456448 | tf_op jit(solution)/shard_map/all_gather | solution.py:12
  9.1 3.2 %copy-start.7 = (f32[1,512]{1,0:T(1,128)S(1)}, f32[1,512]{1,0:T(1,128)}, u32[]{:S(2)}) copy-start(f32[1,512]{1,0:T(1,128)} %param.15) | copy-start | bytes 6148
  9.1 3.2 %copy-start.3 = (f32[1,128,512]{2,1,0:T(8,128)S(1)}, f32[1,128,512]{2,1,0:T(8,128)}, u32[]{:S(2)}) copy-start(f32[1,128,512]{2,1,0:T(8,128)} %param.10) | copy-start | bytes 786436
  16.1 137.6 %all-gather.14.cloned.1.call-start = ((), (), s32[]{:S(2)}) async-start(), calls=%async_computation.2 | async-start | bytes 4456448 | tf_op jit(solution)/shard_map/all_gather | solution.py:12
  88.5 2.9 %copy-start.8 = (bf16[2,2048,512]{2,1,0:T(8,128)(2,1)S(1)}, bf16[2,2048,512]{2,1,0:T(8,128)(2,1)}, u32[]{:S(2)}) copy-start(bf16[2,2048,512]{2,1,0:T(8,128)(2,1)} %param.14) | copy-start | bytes 12582916
  88.6 14.0 %copy-start = (f32[128,512]{1,0:T(8,128)}, f32[128,512]{1,0:T(8,128)S(1)}, u32[]{:S(2)}) copy-start(f32[128,512]{1,0:T(8,128)S(1)} %get-tuple-element.291) | copy-start | bytes 786436
  91.4 2.2 copy-start.1
  91.4 2.7 %copy-start.4 = (f32[1,128,512]{2,1,0:T(8,128)S(1)}, f32[1,128,512]{2,1,0:T(8,128)}, u32[]{:S(2)}) copy-start(f32[1,128,512]{2,1,0:T(8,128)} %param.11) | copy-start | bytes 786436
  97.9 0.7 copy-start.6
  104.5 97.1 %all-gather.10.cloned.1.call-start = ((), (), s32[]{:S(2)}) async-start(), calls=%async_computation | async-start | bytes 3145728 | tf_op jit(solution)/shard_map/all_gather | solution.py:124
  125.4 102.8 %all-gather.16.cloned.1.call-start = ((), (), s32[]{:S(2)}) async-start(), calls=%async_computation.3 | async-start | bytes 3145728 | tf_op jit(solution)/shard_map/all_gather | solution.py:122
  173.0 3.9 %copy-start.5 = (f32[128,512]{1,0:T(8,128)}, f32[128,512]{1,0:T(8,128)S(1)}, u32[]{:S(2)}) copy-start(f32[128,512]{1,0:T(8,128)S(1)} %get-tuple-element.289) | copy-start | bytes 786436
  173.1 2.9 %copy-start.2 = (bf16[2,512,2048]{2,1,0:T(8,128)(2,1)S(1)}, bf16[2,512,2048]{2,1,0:T(8,128)(2,1)}, u32[]{:S(2)}) copy-start(bf16[2,512,2048]{2,1,0:T(8,128)(2,1)} %param.13) | copy-start | bytes 12582916
  176.0 2.2 copy-start.9
Sparse Core Ops, SparseCore 0:
  16.2 53.0 all-gather.11
  104.6 48.9 all-gather.13
  155.8 35.0 all-gather.9
  192.9 35.2 all-gather.15
